TPU v7x, 512 devices: a whole 4x4x16 slice. The times are simulated.
512 devices in a mesh: seq: 128 (over y, x_hi, z), coal: 4 (over x_lo, core).
Axes of the slice: x: 4 (x_hi: 2, x_lo: 2; x = x_hi * 2 + x_lo), y: 4, z: 16, core: 2. Of those that a mesh axis runs over, the one named last changes fastest.
Arguments:
- lat_q: bfloat16 [1024, 1536], P('seq'), may hold values from -4.5 to 4.5
- lat_k: bfloat16 [1024, 1536], P('seq'), may hold values from -4.5 to 4.5
- lat_v: bfloat16 [1024, 1536], P('seq'), may hold values from -6 to 6
- txt_q: bfloat16 [512, 1536], P('seq'), may hold values from -4.5 to 4.5
- txt_k: bfloat16 [512, 1536], P('seq'), may hold values from -4.5 to 4.5
- txt_v: bfloat16 [512, 1536], P('seq'), may hold values from -6 to 6
- span_ids: int32 [512], P('seq'), may hold values from 0 to 15, never falling along the last dimension, each value on 1 to 128 neighbouring positions
- coal_bits: int32 [32], P('coal'), may hold values from 0 to 65535
Outputs:
- txt_out: bfloat16 [32, 512, 1536], P('coal', 'seq')
- lat_out: bfloat16 [32, 1024, 1536], P('coal', 'seq')
Inputs may be any that keep to these rules, and one draw needn't show every extreme that they name: `span_ids`: span ids never fall along the text tokens; each of the 16 spans has one token or more, and the longest has 128.
All inputs are finite; a program needn't handle non-finite values.
Results may differ from a plain program's by a relative error of at most 0.0049.
Values may be sent and summed in bfloat16 or wider, within the bound.
A program may use at most 64 MiB of HBM per device.

v0:
```python
import math

import jax
import jax.numpy as jnp
from jax import lax
from jax.sharding import PartitionSpec as P

HEADS = 12


masked_score = -1e30


def score_block(queries, key_rows, head_count):
    head_size = queries.shape[-1]
    split_keys = key_rows.reshape(key_rows.shape[0], head_count, head_size)
    scaling = 1.0 / math.sqrt(head_size)
    return (
        jnp.einsum("qhd,khd->hqk", queries, split_keys, preferred_element_type=jnp.float32)
        * scaling
    )


def absorb_shared(carried, queries, key_rows, value_rows, head_count):
    old_max, old_sum, old_acc = carried
    scores = score_block(queries, key_rows, head_count)
    new_max = jnp.maximum(old_max, jnp.max(scores, axis=-1))
    weights = jnp.exp(scores - new_max[..., None])
    split_values = value_rows.reshape(value_rows.shape[0], head_count, queries.shape[-1])
    new_sum = jnp.sum(weights, axis=-1)
    product = jnp.einsum(
        "hqk,khd->hqd",
        weights.astype(jnp.bfloat16),
        split_values,
        preferred_element_type=jnp.float32,
    )
    return (new_max, new_sum, product)


def text_stats(queries, key_rows, value_rows, allowed, head_count):
    scores = score_block(queries, key_rows, head_count)
    visible = allowed[:, None, None, :]
    masked = jnp.where(visible, scores[None], masked_score)
    maxima = jnp.max(masked, axis=-1)
    weights = jnp.where(visible, jnp.exp(masked - maxima[..., None]), 0.0)
    split_values = value_rows.reshape(value_rows.shape[0], head_count, queries.shape[-1])
    product = jnp.einsum(
        "chqk,khd->chqd",
        weights.astype(jnp.bfloat16),
        split_values,
        preferred_element_type=jnp.float32,
    )
    return (maxima, jnp.sum(weights, axis=-1), product)


def combine(former, latter):
    joint = jnp.maximum(former[0], latter[0])
    early = jnp.exp(former[0] - joint)
    later = jnp.exp(latter[0] - joint)
    return (
        joint,
        former[1] * early + latter[1] * later,
        former[2] * early[..., None] + latter[2] * later[..., None],
    )


def empty_state(head_count, query_count, head_size):
    return (
        jnp.full((head_count, query_count), masked_score, jnp.float32),
        jnp.zeros((head_count, query_count), jnp.float32),
        jnp.zeros((head_count, query_count, head_size), jnp.float32),
    )


def lifted(carried):
    return (carried[0][None], carried[1][None], carried[2][None])


def finish(carried, own_text):
    outputs = carried[2] / carried[1][..., None]
    coal_count, head_count, query_count, head_size = outputs.shape
    merged = jnp.transpose(outputs, (0, 2, 1, 3)).reshape(
        coal_count, query_count, head_count * head_size
    )
    merged = merged.astype(jnp.bfloat16)
    return (merged[:, :own_text], merged[:, own_text:])


def per_device(lat_q, lat_k, lat_v, txt_q, txt_k, txt_v, span_ids, coal_bits):
    head_count = HEADS
    own_text = txt_q.shape[0]
    queries = jnp.concatenate([txt_q, lat_q], axis=0)
    query_count = queries.shape[0]
    split_q = queries.reshape(query_count, head_count, -1)
    head_size = split_q.shape[-1]
    kept_marks = (jnp.right_shift(coal_bits[None, :], span_ids[:, None]) & 1).astype(jnp.bfloat16)
    text_keys, text_values, all_marks = (
        lax.all_gather(txt_k, "seq", axis=0, tiled=True),
        lax.all_gather(txt_v, "seq", axis=0, tiled=True),
        lax.all_gather(kept_marks, "seq", axis=0, tiled=True),
    )
    allowed = jnp.transpose(all_marks) > 0.5
    text_part = text_stats(split_q, text_keys, text_values, allowed, head_count)
    shared = absorb_shared(
        empty_state(head_count, query_count, head_size),
        split_q,
        lax.all_gather(lat_k, "seq", axis=0, tiled=True),
        lax.all_gather(lat_v, "seq", axis=0, tiled=True),
        head_count,
    )
    final_state = combine(lifted(shared), text_part)
    return finish(final_state, own_text)


def solution(mesh):
    return jax.shard_map(
        per_device,
        mesh=mesh,
        in_specs=(
            P("seq", None),
            P("seq", None),
            P("seq", None),
            P("seq", None),
            P("seq", None),
            P("seq", None),
            P("seq"),
            P("coal"),
        ),
        out_specs=(P("coal", "seq", None), P("coal", "seq", None)),
        check_vma=False,
    )
```

profile of v0, /device:TPU:1, one launch (start us, length us, event | category | flops | bytes accessed | tf_op | source)
XLA Modules:
  0.0 854.0 jit_solution(1025637901350506341)
XLA Ops:
  7.2 0.0 all-gather.12.cloned.1.call-start
  7.2 0.7 all-gather.12.cloned.1.call-update
  7.9 0.0 all-gather.14.cloned.1.call-start
  7.9 0.7 all-gather.14.cloned.1.call-update
  8.6 0.0 all-gather.8.cloned.1.call-start
  8.7 0.7 all-gather.8.cloned.1.call-update
  9.4 0.0 all-gather.10.cloned.1.call-start
  9.4 0.5 all-gather.10.cloned.1.call-update
  10.0 0.8 pad_maximum_fusion
  10.7 0.1 reshape.50
  10.8 0.0 copy-start.2
  10.8 0.8 fusion.51
  11.6 307.0 %all-gather = bf16[128,4,8]{2,1,0:T(4,128)(2,1)S(1)} all-gather(bf16[1,4,8]{2,1,0:T(4,128)(2,1)S(1)} %fusion.51), channel_id=1, replica_groups=mesh['seq'=128,'coal'=4] {'seq'}, dimensions={0}, use_global_device_ids=true | all-gather | bytes 8256 | tf_op jit(solution)/shard_map/all_gather | solution.py:100
  318.6 0.1 broadcast_compare_fusion
  318.6 0.1 copy.28
  318.7 0.0 copy-start.7
  318.7 0.0 all-gather.12.cloned.1.call-done
  318.8 3.2 reshape.53
  322.0 81.2 %all-gather.14.cloned.1.call-done = bf16[128,4,1536]{2,1,0:T(4,128)(2,1)} async-done(((bf16[1,4,1536]{2,1,0:T(4,128)(2,1)}), bf16[128,4,1536]{2,1,0:T(4,128)(2,1)}) %all-gather.14.cloned.1.call-update) | async-done | bytes 1572880 | tf_op jit(solution)/shard_map/all_gather | solution.py:99
  403.1 4.2 reshape.54
  407.4 0.0 copy-done.2
  407.4 0.7 fusion.29
  408.0 0.5 select_reduce_fusion
  408.5 0.0 copy-done.7
  408.5 0.0 copy-start.3
  408.5 0.6 copy-done.3
  409.1 1.7 fusion.2
  410.8 210.1 %all-gather.8.cloned.1.call-done = bf16[1024,1536]{1,0:T(8,128)(2,1)} async-done(((bf16[8,1536]{1,0:T(8,128)(2,1)}), bf16[1024,1536]{1,0:T(8,128)(2,1)}) %all-gather.8.cloned.1.call-update) | async-done | bytes 3145744 | tf_op jit(solution)/shard_map/all_gather | solution.py:107
  621.0 3.2 copy.23
  624.2 1.4 fusion.57
  625.6 0.0 copy-start
  625.6 0.7 fusion.54
  626.2 0.3 copy-done
  626.5 0.3 fusion.42
  626.7 211.6 %all-gather.10.cloned.1.call-done = bf16[1024,1536]{1,0:T(8,128)(2,1)} async-done(((bf16[8,1536]{1,0:T(8,128)(2,1)}), bf16[1024,1536]{1,0:T(8,128)(2,1)}) %all-gather.10.cloned.1.call-update) | async-done | bytes 3145744 | tf_op jit(solution)/shard_map/all_gather | solution.py:108
  838.4 3.2 copy.26
  841.6 0.0 copy-start.4
  841.6 0.0 copy-start.5
  841.6 0.0 copy-start.6
  841.6 0.0 copy-start.1
  841.6 0.0 copy-start.8
  841.6 2.2 convolution_bitcast_fusion
  843.9 0.0 copy-done.4
  843.9 0.0 copy-done.5
  843.9 0.0 copy-done.6
  843.9 0.0 copy-done.1
  844.0 0.0 copy-done.8
  844.0 1.9 fusion.37
  845.9 0.1 copy.63
  846.0 0.7 copy.34
  846.8 0.7 copy.33
  (3 shorter events, 0.1 us)
Async XLA Ops:
  7.2 311.6 %all-gather.12.cloned.1.call-start = ((), (), s32[]{:S(2)}) async-start(), calls=%async_computation.2 | async-start | bytes 1585152 | tf_op jit(solution)/shard_map/all_gather | solution.py:98
  7.9 395.2 %all-gather.14.cloned.1.call-start = ((), (), s32[]{:S(2)}) async-start(), calls=%async_computation.3 | async-start | bytes 1585152 | tf_op jit(solution)/shard_map/all_gather | solution.py:99
  8.6 612.3 %all-gather.8.cloned.1.call-start = ((), (), s32[]{:S(2)}) async-start(), calls=%async_computation | async-start | bytes 3170304 | tf_op jit(solution)/shard_map/all_gather | solution.py:107
  9.4 829.0 %all-gather.10.cloned.1.call-start = ((), (), s32[]{:S(2)}) async-start(), calls=%async_computation.1 | async-start | bytes 3170304 | tf_op jit(solution)/shard_map/all_gather | solution.py:108
  10.8 396.6 %copy-start.2 = (bf16[12,12,128]{2,1,0:T(8,128)(2,1)}, bf16[12,12,128]{2,1,0:T(8,128)(2,1)S(1)}, u32[]{:S(2)}) copy-start(bf16[12,12,128]{2,1,0:T(8,128)(2,1)S(1)} %reshape.50) | copy-start | bytes 110596
  318.7 89.8 %copy-start.7 = (pred[8,512]{1,0:T(8,128)(4,1)}, pred[8,512]{1,0:T(8,128)(4,1)S(1)}, u32[]{:S(2)}) copy-start(pred[8,512]{1,0:T(8,128)(4,1)S(1)} %copy.28) | copy-start | bytes 12292
  408.5 0.6 copy-start.3
  625.6 0.9 copy-start
  841.6 2.3 copy-start.4
  841.6 2.3 copy-start.5
  841.6 2.3 copy-start.6
  841.6 2.3 copy-start.1
  841.6 2.3 copy-start.8
Sparse Core Ops, SparseCore 0:
  12.3 194.1 all-gather.11
  210.8 192.3 all-gather.13
  407.7 213.2 all-gather.7
  625.4 212.9 all-gather.9
where the time goes:
time: 863 us; the launch traced here: 854 us
  waiting for transfers between devices  506 us (59%)
  blocking collectives  307 us (36%)
  local copies, waits for them, and re-layouts  16.4 us (2%)
  between operations  13.9 us (2%)
    all_gather x1, blocking collectives, per_device(): lax.all_gather(kept_marks, 'seq', axis=0, tiled=True)  307 us
    all_gather x1, waiting for transfers between devices, per_device(): lax.all_gather(lat_v, 'seq', axis=0, tiled=True)  212 us
    all_gather x1, waiting for transfers between devices, per_device(): lax.all_gather(lat_k, 'seq', axis=0, tiled=True)  210 us
    all_gather x1, waiting for transfers between devices, per_device(): lax.all_gather(txt_v, 'seq', axis=0, tiled=True)  81.2 us
  transfers between devices with their start and end apart: 4, of which 3 were waited for; matrix products, arithmetic and copies ran while one was open for 2% of the time, Pallas kernels for 0%

commit v1 on v0

v1 whole, which is shorter than its diff:
```python
import functools
import math

import jax
import jax.numpy as jnp
from jax import lax
from jax.experimental import pallas as pl
from jax.experimental.pallas import tpu as pltpu
from jax.sharding import PartitionSpec as P

MESH = pl.DeviceIdType.MESH
BF16, F32 = jnp.bfloat16, jnp.float32

YS, XS, ZS = 4, 4, 16
ROWS_Y = 3
HD = 128
SCALE2 = math.log2(math.e) / math.sqrt(HD)
HIDDEN = -1e30
UNITS = 13
FAR = 5


def place():
    seq, coal = lax.axis_index("seq"), lax.axis_index("coal")
    return lax.div(seq, 32), lax.rem(lax.div(seq, 16), 2), lax.rem(seq, 16), lax.div(coal, 2), lax.rem(coal, 2)


def device(y, x, z, core):
    return ((y * 2 + lax.div(x, 2)) * ZS + z, lax.rem(x, 2) * 2 + core)


def widened(unit):
    return unit.astype(F32)


def kernel(
    spans, bits, lq, lk, lv, tq, tk, tv, out_t, out_l,
    own, queries, biases, gathered, text_k, text_v, lat_k, lat_v, bias_rows, base_q, lat_stats, lat_mixed, results, landed,
    s0_send, s0_recv, q0_send, q0_recv, b_send, b_recv, z_send, z_recv, c_send, c_recv, o_send, o_recv,
):
    y, x_hi, z, x_lo, core = place()
    x = x_hi * 2 + x_lo
    coal = x_lo * 2 + core
    active = y < ROWS_Y

    def at_z(shift):
        return device(y, x, lax.rem(z + shift + ZS, ZS), core)

    barrier = pltpu.get_barrier_semaphore()
    partners = []
    for dy in range(YS):
        for dx in range(XS):
            for dc in range(2):
                if dy or dx or dc:
                    partners.append(
                        device(lax.rem(y + dy, YS), lax.rem(x + dx, XS), z, lax.rem(core + dc, 2))
                    )
    for shift in (1, 2, 3, FAR):
        partners.append(at_z(shift))
        partners.append(at_z(-shift))
    for partner in partners:
        pl.semaphore_signal(barrier, inc=1, device_id=partner, device_id_type=MESH)

    sub = lax.broadcasted_iota(jnp.int32, (8, HD), 0)
    lane = lax.broadcasted_iota(jnp.int32, (8, HD), 1)
    upper = sub < 4
    x_to = jnp.where(core == 0, x, jnp.where(x_lo == 0, lax.rem(x + 3, XS), lax.rem(x + 1, XS)))
    span = jnp.zeros((8, HD), jnp.int32)
    for row in range(4):
        span = jnp.where(sub == 4 + row, spans[row], span)
    one_hot = jnp.where((lane == span + 16 * lax.div(y, 2)), 1.0, 0.0)
    for y_to in range(ROWS_Y):
        cols = pl.ds(pl.multiple_of((x_to * ROWS_Y + y_to) * HD, HD), HD)
        own[y_to, 0] = jnp.concatenate([widened(tk[:, cols]), widened(tv[:, cols])], axis=0).astype(BF16)
        own[y_to, 1] = lk[:, cols]
        own[y_to, 2] = lv[:, cols]
        asked = widened(tq[:, cols])
        own[y_to, 3] = jnp.where(upper, jnp.concatenate([asked, asked], axis=0), one_hot).astype(BF16)
        own[y_to, 4] = lq[:, cols]
    kept = jnp.zeros((8, HD), jnp.int32)
    for row in range(8):
        kept = jnp.where(sub == row, bits[row], kept)
    shown = jnp.right_shift(kept, jnp.bitwise_and(lane, 15)) & 1
    biases[coal] = jnp.where((lane < 32) & (shown == 0), HIDDEN, 0.0).astype(BF16)
    text_v[:, HD:] = jnp.ones((512, HD), BF16)
    lat_v[:, HD:] = jnp.ones((1024, HD), BF16)

    pl.semaphore_wait(barrier, len(partners))

    def rows_to(y_to):
        target = device(jnp.int32(y_to), x_to, z, x_hi)
        return [
            (own.at[y_to, pl.ds(0, 3)], gathered.at[0, x_hi, pl.ds(y * 3, 3)], s0_send.at[y_to], s0_recv.at[y], target),
            (own.at[y_to, pl.ds(3, 2)], queries.at[y], q0_send.at[y_to], q0_recv.at[y], target),
        ]

    def remote(src, dst, send, recv, target):
        return pltpu.make_async_remote_copy(
            src_ref=src, dst_ref=dst, send_sem=send, recv_sem=recv, device_id=target, device_id_type=MESH
        )

    for y_to in range(ROWS_Y):
        to_self = (core == 0) & (x_hi == 0) & (y == y_to)
        for src, dst, send, recv, target in rows_to(y_to):

            @pl.when(to_self)
            def _():
                pltpu.make_async_copy(src, dst, recv).start()

            @pl.when(jnp.logical_not(to_self))
            def _():
                remote(src, dst, send, recv, target).start()

    def bias_copies():
        chip = x_hi * 2 + 1 - x_lo
        for n, target in enumerate((device(y, x, z, 1 - core), device(y, chip, z, core), device(y, chip, z, 1 - core))):
            yield remote(biases.at[coal], biases.at[coal], b_send.at[n], b_recv.at[coal], target)

    def ring(offset, shift, n, first=0, count=UNITS):
        here = gathered.at[offset % ZS, core, pl.ds(first, count)]
        there = gathered.at[(offset - shift) % ZS, core, pl.ds(first, count)]
        return remote(here, there, z_send.at[n], z_recv.at[n], at_z(shift))

    def across(offset):
        block = gathered.at[offset % ZS, core]
        return remote(block, block, c_send.at[offset % ZS], c_recv.at[offset % ZS], device(y, x, z, 1 - core))

    half = UNITS // 2
    stage_one = [(0, FAR), (0, -FAR), (0, 1), (0, -1), (0, 2), (0, -2)]
    stage_two = [
        (FAR, -3, half, UNITS - half), (-FAR, 3, 0, half),
        (FAR, 1), (FAR, -1), (-FAR, 1), (-FAR, -1), (FAR, 2), (FAR, -2), (-FAR, 2), (-FAR, -2),
    ]

    def stage_one_copies():
        return [ring(o, s, n) for n, (o, s) in enumerate(stage_one)]

    def stage_two_copies():
        return [ring(c[0], c[1], len(stage_one) + n, *c[2:]) for n, c in enumerate(stage_two)]

    def converted(o):
        for k in range(2):
            part = [widened(gathered[o, k, n]) for n in range(UNITS)]
            keys, values = [], []
            for pair in range(2):
                one, two = part[pair * 6], part[pair * 6 + 3]
                keys.append(jnp.where(upper, one, pltpu.roll(two, 4, 0)))
                values.append(jnp.where(upper, pltpu.roll(one, 4, 0), two))
            marks = [jnp.where(lane < 16, part[12], 0.0), jnp.where(lane < 16, 0.0, part[12])]
            rows = pl.ds((o * 2 + k) * 16, 16)
            text_k[rows, pl.ds(0, HD)] = jnp.concatenate(keys, axis=0).astype(BF16)
            text_k[rows, pl.ds(HD, HD)] = jnp.concatenate(marks, axis=0).astype(BF16)
            text_v[rows, pl.ds(0, HD)] = jnp.concatenate(values, axis=0).astype(BF16)
            rows = pl.ds((o * 2 + k) * 32, 32)
            lat_k[rows, :] = jnp.concatenate([part[n * 3 + 1] for n in range(4)], axis=0).astype(BF16)
            lat_v[rows, pl.ds(0, HD)] = jnp.concatenate([part[n * 3 + 2] for n in range(4)], axis=0).astype(BF16)

    nt = (((1,), (1,)), ((), ()))

    @pl.when(active)
    def _():
        for copy in bias_copies():
            copy.start()
        for n in range(YS):
            pltpu.make_async_copy(queries.at[n], queries.at[n], q0_recv.at[n]).wait()
        units = [widened(queries[n, 0]) for n in range(YS)]
        marks = [jnp.where(upper, pltpu.roll(units[n], 4, 0), units[n + 1]) for n in (0, 2)]
        own_marks = jnp.where(lane < 16, marks[0], marks[1])
        gathered[0, core, 12] = own_marks.astype(BF16)
        for n in range(YS):
            block = gathered.at[0, core, pl.ds(n * 3, 3)]
            pltpu.make_async_copy(block, block, s0_recv.at[n]).wait()
        first = stage_one_copies()
        for copy in first:
            copy.start()
        crossing = [across(o) for o in range(ZS)]
        crossing[0].start()

        for n in range(YS):
            twice = jnp.where(upper, units[n], pltpu.roll(units[n], 4, 0))
            base_q[pl.ds(n * 16, 16), :] = jnp.concatenate([twice, widened(queries[n, 1])], axis=0).astype(BF16)

        second = stage_two_copies()
        for n, fast in ((0, (1, 6, 7, 8, 9)), (1, (0, 2, 3, 4, 5))):
            first[n].wait_recv()
        for copy in second:
            copy.start()
        crossing[FAR].start()
        crossing[ZS - FAR].start()
        for n in range(2, 6):
            first[n].wait_recv()
            crossing[-stage_one[n][1] % ZS].start()
        for g in range(4):

            @pl.when(coal != g)
            def _():
                pltpu.make_async_copy(biases.at[g], biases.at[g], b_recv.at[g]).wait()

            unit = widened(biases[g])
            rows = [unit[c : c + 1, :] for c in range(8)]
            parts = [jnp.where(upper, rows[2 * p], rows[2 * p + 1]) for p in range(4)]
            parts += [jnp.broadcast_to(row, (8, HD)) for row in rows]
            bias_rows[g] = jnp.concatenate(parts, axis=0).astype(BF16)
        second[0].wait_recv()
        second[1].wait_recv()
        crossing[8].start()
        for n in range(2, 10):
            second[n].wait_recv()
            crossing[(stage_two[n][0] - stage_two[n][1]) % ZS].start()
        for o in range(ZS):
            crossing[o].wait_recv()
            converted(o)

        scores = lax.dot_general(base_q[...], lat_k[...], nt, preferred_element_type=F32) * SCALE2
        maxima = jnp.max(scores, axis=1, keepdims=True)
        weights = jnp.exp2(scores - maxima).astype(BF16)
        lat_stats[...] = jnp.broadcast_to(maxima, (64, HD))
        lat_mixed[...] = jnp.dot(weights, lat_v[...], preferred_element_type=F32)

        head = x * ROWS_Y + y

        def to_device(step):
            row, g = lax.div(step, 4), lax.rem(step, 4)
            target = (((row * 2 + core) * ZS + z), g)
            return (
                (row == y) & (core == x_hi) & (g == coal),
                remote(results.at[step], landed.at[head], o_send.at[step], o_recv.at[head], target),
            )

        def spread(text, latent):
            return jnp.concatenate([text] * 4 + [latent] * 8, axis=0)

        def one_device(step, _):
            row, g = lax.div(step, 4), lax.rem(step, 4)
            at_text = pl.ds(pl.multiple_of(row * 16, 16), 8)
            at_latent = pl.ds(pl.multiple_of(row * 16 + 8, 8), 8)
            asked = base_q[pl.ds(pl.multiple_of(row * 16, 16), 16), :].astype(F32)
            left = spread(asked[:8], asked[8:]).astype(BF16)
            full = jnp.concatenate([left, bias_rows[g]], axis=1)
            scores = lax.dot_general(full, text_k[...], nt, preferred_element_type=F32) * SCALE2
            shared = spread(lat_stats[at_text, :], lat_stats[at_latent, :])[:, :1]
            maxima = jnp.maximum(jnp.max(scores, axis=1, keepdims=True), shared)
            weights = jnp.exp2(scores - maxima).astype(BF16)
            total = jnp.dot(weights, text_v[...], preferred_element_type=F32)
            total = total + jnp.exp2(shared - maxima) * spread(lat_mixed[at_text, :], lat_mixed[at_latent, :])
            results[step] = (total[:, :HD] / total[:, HD:]).astype(BF16)
            to_self, copy = to_device(step)

            @pl.when(to_self)
            def _():
                pltpu.make_async_copy(results.at[step], landed.at[head], o_recv.at[head]).start()

            @pl.when(jnp.logical_not(to_self))
            def _():
                copy.start()

            return 0

        lax.fori_loop(0, 16, one_device, 0)

        for copy in first + second:
            copy.wait_send()
        for copy in crossing:
            copy.wait_send()
        for copy in bias_copies():
            copy.wait_send()

        def drained(step, _):
            to_self, copy = to_device(step)

            @pl.when(jnp.logical_not(to_self))
            def _():
                copy.wait_send()

            return 0

        lax.fori_loop(0, 16, drained, 0)

    for y_to in range(ROWS_Y):
        to_self = (core == 0) & (x_hi == 0) & (y == y_to)
        for src, dst, send, recv, target in rows_to(y_to):

            @pl.when(jnp.logical_not(to_self))
            def _():
                remote(src, dst, send, recv, target).wait_send()

    for head in range(ROWS_Y * XS):
        pltpu.make_async_copy(landed.at[head], landed.at[head], o_recv.at[head]).wait()
        out_t[:, head * HD : (head + 1) * HD] = landed[head, :32]
        out_l[:, head * HD : (head + 1) * HD] = landed[head, 32:]


def per_device(lat_q, lat_k, lat_v, txt_q, txt_k, txt_v, span_ids, coal_bits):
    vmem = pl.BlockSpec(memory_space=pltpu.VMEM)
    smem = pl.BlockSpec(memory_space=pltpu.SMEM)
    dma = pltpu.SemaphoreType.DMA
    out_t, out_l = pl.pallas_call(
        kernel,
        out_shape=(jax.ShapeDtypeStruct((32, 1536), BF16), jax.ShapeDtypeStruct((64, 1536), BF16)),
        in_specs=[smem, smem] + [vmem] * 6,
        out_specs=(vmem, vmem),
        scratch_shapes=[
            pltpu.VMEM((ROWS_Y, 5, 8, HD), BF16),
            pltpu.VMEM((YS, 2, 8, HD), BF16),
            pltpu.VMEM((4, 8, HD), BF16),
            pltpu.VMEM((ZS, 2, UNITS, 8, HD), BF16),
            pltpu.VMEM((512, 2 * HD), BF16),
            pltpu.VMEM((512, 2 * HD), BF16),
            pltpu.VMEM((1024, HD), BF16),
            pltpu.VMEM((1024, 2 * HD), BF16),
            pltpu.VMEM((4, 96, HD), BF16),
            pltpu.VMEM((64, HD), BF16),
            pltpu.VMEM((64, HD), F32),
            pltpu.VMEM((64, 2 * HD), F32),
            pltpu.VMEM((16, 96, HD), BF16),
            pltpu.VMEM((12, 96, HD), BF16),
            dma((3,)), dma((4,)), dma((3,)), dma((4,)), dma((3,)), dma((4,)),
            dma((16,)), dma((16,)), dma((16,)), dma((16,)), dma((16,)), dma((12,)),
        ],
        compiler_params=pltpu.CompilerParams(collective_id=0, has_side_effects=True),
        name="coalition_attention",
    )(span_ids, coal_bits, lat_q, lat_k, lat_v, txt_q, txt_k, txt_v)
    return out_t.reshape(8, 4, 1536), out_l.reshape(8, 8, 1536)


def solution(mesh):
    return jax.shard_map(
        per_device,
        mesh=mesh,
        in_specs=(P("seq", None),) * 6 + (P("seq"), P("coal")),
        out_specs=(P("coal", "seq", None), P("coal", "seq", None)),
        check_vma=False,
    )
```

time: 863 us -> 50.8 us (0.06)
  the two profiles are of different devices: /device:TPU:1 before, /device:TPU:63 now
where the time goes in v1:
time: 50.8 us; the launch traced here: 50.6 us
  Pallas kernels  47.6 us (94%)
  local copies, waits for them, and re-layouts  2.28 us (4%)
  between operations  0.65 us (1%)
    pallas_call x1, Pallas kernels, per_device(): pl.pallas_call(kernel, out_shape=(jax.ShapeDtypeStruct((32, 1536), BF16),...  47.6 us
    reshape x1, local copies, waits for them, and re-layouts, per_device(): return (out_t.reshape(8, 4, 1536), out_l.reshape(8, 8, 1536))  1.6 us

profile of v1, /device:TPU:63, one launch (start us, length us, event | category | flops | bytes accessed | tf_op | source)
XLA Modules:
  0.0 50.6 jit_solution(8344729999896943700)
XLA Ops:
  0.6 47.6 %coalition_attention.1 = (bf16[32,1536]{1,0:T(8,128)(2,1)}, bf16[64,1536]{1,0:T(8,128)(2,1)}) custom-call(s32[4]{0:T(128)} %spans.1, s32[8]{0:T(128)} %bits.1, bf16[8,1536]{1,0:T(8,128)(2,1)} %lq.1, bf16[8,1536]{1,0:T(8,128)(2,1)} %lk.1, bf16[8,1536]{1,0:T(8,128)(2,1)} %lv.1, bf16[4,1536]{1,0:T(4,128)(2,1)} %tq.1, bf16[4,1536]{1,0:T(4,128)(2,1)} %tk.1, ...), custom_call_target="tpu_custom_call" | custom-call | tf_op jit(solution)/shard_map/coalition_attention/pallas_call | solution.py:297
  48.3 0.0 copy-start
  48.3 1.6 %reshape.10 = bf16[8,4,1536]{2,1,0:T(4,128)(2,1)} reshape(bf16[32,1536]{1,0:T(8,128)(2,1)} %get-tuple-element.4) | data formatting | bytes 196608 | tf_op jit(solution)/shard_map/reshape | solution.py:323
  49.9 0.0 copy-done
  49.9 0.7 %copy.11 = bf16[8,8,1536]{2,1,0:T(8,128)(2,1)} copy(bf16[8,8,1536]{2,1,0:T(8,128)(2,1)S(1)} %bitcast.1) | data formatting | bytes 393216
Async XLA Ops:
  48.3 1.6 %copy-start = (bf16[64,1536]{1,0:T(8,128)(2,1)S(1)}, bf16[64,1536]{1,0:T(8,128)(2,1)}, u32[]{:S(2)}) copy-start(bf16[64,1536]{1,0:T(8,128)(2,1)} %get-tuple-element.5) | copy-start | bytes 589828

commit v2 on v1

v2 whole, which is shorter than its diff:
```python
import functools
import math

import jax
import jax.numpy as jnp
from jax import lax
from jax.experimental import pallas as pl
from jax.experimental.pallas import tpu as pltpu
from jax.sharding import PartitionSpec as P

MESH = pl.DeviceIdType.MESH
BF16, F32 = jnp.bfloat16, jnp.float32

YS, XS, ZS = 4, 4, 16
ROWS_Y = 3
HD = 128
SCALE2 = math.log2(math.e) / math.sqrt(HD)
HIDDEN = -1e30
PARTS = 7
FAR = 5
SHIFTS = (FAR, -FAR, 2, -2, 1, -1, 0)


def place():
    seq, coal = lax.axis_index("seq"), lax.axis_index("coal")
    return lax.div(seq, 32), lax.rem(lax.div(seq, 16), 2), lax.rem(seq, 16), lax.div(coal, 2), lax.rem(coal, 2)


def device(y, x, z, core):
    return ((y * 2 + lax.div(x, 2)) * ZS + z, lax.rem(x, 2) * 2 + core)


def widened(unit):
    return unit.astype(F32)


def kernel(
    spans_in, bits_in, lq_in, lk_in, lv_in, tq_in, tk_in, tv_in, landed,
    spans, bits, lq, lk, lv, tq, tk, tv,
    own, own_q, queries, biases, gathered, text_k, text_v, lat_k, lat_v, bias_rows, base_q, lat_stats, lat_mixed, results,
    in_sem, s_send, s_recv, q_send, q_recv, b_send, b_recv, z_send, z_recv, c_send, c_recv, o_send, o_recv,
):
    y, x_hi, z, x_lo, core = place()
    x = x_hi * 2 + x_lo
    coal = x_lo * 2 + core
    active = y < ROWS_Y

    def at_z(shift):
        return device(y, x, lax.rem(z + shift + ZS, ZS), core)

    loads = [
        pltpu.make_async_copy(src, dst, in_sem.at[n])
        for n, (src, dst) in enumerate(
            ((spans_in, spans), (bits_in, bits), (tk_in, tk), (tv_in, tv), (lk_in, lk), (lv_in, lv), (tq_in, tq), (lq_in, lq))
        )
    ]
    for load in loads:
        load.start()

    barrier = pltpu.get_barrier_semaphore()

    def greet(partner):
        pl.semaphore_signal(barrier, inc=1, device_id=partner, device_id_type=MESH)

    x_from = jnp.where(core == x_hi, x, jnp.where(x_lo == 0, lax.rem(x + 3, XS), lax.rem(x + 1, XS)))
    core_from = jnp.where(core == x_hi, 0, 1)
    other_chip = x_hi * 2 + 1 - x_lo
    others = (device(y, x, z, 1 - core), device(y, other_chip, z, core), device(y, other_chip, z, 1 - core))

    @pl.when(active)
    def _():
        for shift in SHIFTS:
            for y_from in range(YS):
                source = device(jnp.int32(y_from), x_from, lax.rem(z - shift + ZS, ZS), core_from)
                if shift:
                    greet(source)
                else:

                    @pl.when(jnp.logical_not((y == y_from) & (core == x_hi) & (core == 0)))
                    def _():
                        greet(source)

        for shift in (1, 2, 3):
            greet(at_z(shift))
            greet(at_z(-shift))
        for other in others:
            greet(other)

    for y_from in range(ROWS_Y):
        for x_of in range(XS):

            @pl.when(jnp.logical_not((y == y_from) & (x == x_of) & (core == x_hi)))
            def _():
                greet(device(jnp.int32(y_from), jnp.int32(x_of), z, x_hi))

    for load in loads:
        load.wait()

    sub = lax.broadcasted_iota(jnp.int32, (8, HD), 0)
    lane = lax.broadcasted_iota(jnp.int32, (8, HD), 1)
    upper = sub < 4
    x_to = jnp.where(core == 0, x, jnp.where(x_lo == 0, lax.rem(x + 3, XS), lax.rem(x + 1, XS)))
    span = jnp.zeros((8, HD), jnp.int32)
    for row in range(4):
        span = jnp.where(sub == row, spans[row], span)
    one_hot = jnp.where(lane == span, 1.0, 0.0)[:4]
    for y_to in range(ROWS_Y):
        cols = pl.ds(pl.multiple_of((x_to * ROWS_Y + y_to) * HD, HD), HD)
        keys, values, asked = widened(lk[:, cols]), widened(lv[:, cols]), widened(lq[:, cols])
        own[y_to, 0] = tk[:, cols]
        own[y_to, 1] = tv[:, cols]
        own[y_to, 2] = one_hot.astype(BF16)
        for n in range(2):
            own[y_to, 3 + n] = keys[n * 4 : n * 4 + 4].astype(BF16)
            own[y_to, 5 + n] = values[n * 4 : n * 4 + 4].astype(BF16)
            own_q[y_to, 1 + n] = asked[n * 4 : n * 4 + 4].astype(BF16)
        own_q[y_to, 0] = tq[:, cols]
    kept = jnp.zeros((8, HD), jnp.int32)
    for row in range(8):
        kept = jnp.where(sub == row, bits[row], kept)
    shown = jnp.right_shift(kept, jnp.bitwise_and(lane, 15)) & 1
    biases[coal] = jnp.where((lane < 16) & (shown == 0), HIDDEN, 0.0).astype(BF16)
    text_v[:, HD:] = jnp.ones((512, HD), BF16)
    lat_v[:, HD:] = jnp.ones((1024, HD), BF16)

    in_own = (core == 0) & (x_hi == 0) & active
    awaited = len(SHIFTS) * ROWS_Y - in_own.astype(jnp.int32)
    mine = 6 + 3 + 16 - (core == x_hi).astype(jnp.int32)
    pl.semaphore_wait(barrier, awaited + jnp.where(active, mine, 0))

    def remote(src, dst, send, recv, target):
        return pltpu.make_async_remote_copy(
            src_ref=src, dst_ref=dst, send_sem=send, recv_sem=recv, device_id=target, device_id_type=MESH
        )

    def rows_to(n, y_to):
        target = device(jnp.int32(y_to), x_to, lax.rem(z + SHIFTS[n] + ZS, ZS), x_hi)
        there = gathered.at[-SHIFTS[n] % ZS, x_hi, pl.ds(y * PARTS, PARTS)]
        return (own.at[y_to], there, s_send.at[n * ROWS_Y + y_to], s_recv.at[n * YS + y], target)

    def queries_to(y_to):
        target = device(jnp.int32(y_to), x_to, z, x_hi)
        return (own_q.at[y_to], queries.at[y], q_send.at[y_to], q_recv.at[y], target)

    def maybe_own(y_to, copy):
        src, dst, send, recv, target = copy
        to_self = in_own & (y == y_to)

        @pl.when(to_self)
        def _():
            pltpu.make_async_copy(src, dst, recv).start()

        @pl.when(jnp.logical_not(to_self))
        def _():
            remote(src, dst, send, recv, target).start()

    for n in range(len(SHIFTS)):
        for y_to in range(ROWS_Y):
            if SHIFTS[n]:
                remote(*rows_to(n, y_to)).start()
            else:
                maybe_own(y_to, rows_to(n, y_to))
                maybe_own(y_to, queries_to(y_to))

    def bias_copies():
        for n, target in enumerate(others):
            yield remote(biases.at[coal], biases.at[coal], b_send.at[n], b_recv.at[coal], target)

    whole = YS * PARTS

    def ring(n, offset, shift, first=0, count=whole):
        here = gathered.at[offset % ZS, core, pl.ds(first, count)]
        there = gathered.at[(offset - shift) % ZS, core, pl.ds(first, count)]
        return remote(here, there, z_send.at[n], z_recv.at[n], at_z(shift))

    def across(offset):
        block = gathered.at[offset % ZS, core]
        return remote(block, block, c_send.at[offset % ZS], c_recv.at[offset % ZS], others[0])

    half = whole // 2
    forwards = [
        (FAR, -3, half, whole - half), (-FAR, 3, 0, half),
        (FAR, 2), (FAR, -2), (FAR, 1), (FAR, -1), (-FAR, 2), (-FAR, -2), (-FAR, 1), (-FAR, -1),
    ]

    def direct_in(n):
        for y_from in range(YS):
            block = gathered.at[-SHIFTS[n] % ZS, core, pl.ds(y_from * PARTS, PARTS)]
            pltpu.make_async_copy(block, block, s_recv.at[n * YS + y_from]).wait()

    def converted(o):
        for k in range(2):
            part = [[widened(gathered[o, k, n * PARTS + m]) for m in range(PARTS)] for n in range(YS)]

            def rows_of(*which):
                return jnp.concatenate([part[n][m] for n in range(YS) for m in which], axis=0).astype(BF16)

            rows = pl.ds((o * 2 + k) * 16, 16)
            text_k[rows, pl.ds(0, HD)] = rows_of(0)
            text_k[rows, pl.ds(HD, HD)] = rows_of(2)
            text_v[rows, pl.ds(0, HD)] = rows_of(1)
            rows = pl.ds((o * 2 + k) * 32, 32)
            lat_k[rows, :] = rows_of(3, 4)
            lat_v[rows, pl.ds(0, HD)] = rows_of(5, 6)

    nt = (((1,), (1,)), ((), ()))

    @pl.when(active)
    def _():
        for copy in bias_copies():
            copy.start()
        second = [ring(n, *f) for n, f in enumerate(forwards)]
        crossing = [across(o) for o in range(ZS)]
        for n in (0, 1):
            direct_in(n)
            for f, copy in zip(forwards, second):
                if f[0] == -SHIFTS[n]:
                    copy.start()
            crossing[-SHIFTS[n] % ZS].start()
        for n in range(2, len(SHIFTS)):
            direct_in(n)
            crossing[-SHIFTS[n] % ZS].start()

        for n in range(YS):
            pltpu.make_async_copy(queries.at[n], queries.at[n], q_recv.at[n]).wait()
            asked = [widened(queries[n, m]) for m in (0, 0, 1, 2)]
            base_q[pl.ds(n * 16, 16), :] = jnp.concatenate(asked, axis=0).astype(BF16)
        for g in range(4):

            @pl.when(coal != g)
            def _():
                pltpu.make_async_copy(biases.at[g], biases.at[g], b_recv.at[g]).wait()

            unit = widened(biases[g])
            rows = [unit[c : c + 1, :] for c in range(8)]
            parts = [jnp.where(upper, rows[2 * p], rows[2 * p + 1]) for p in range(4)]
            parts += [jnp.broadcast_to(row, (8, HD)) for row in rows]
            bias_rows[pl.ds(g * 96, 96), :] = jnp.concatenate(parts, axis=0).astype(BF16)
        for shift in SHIFTS:
            crossing[-shift % ZS].wait_recv()
            converted(-shift % ZS)
        for n in range(2, len(forwards)):
            second[n].wait_recv()
            crossing[(forwards[n][0] - forwards[n][1]) % ZS].start()
        second[0].wait_recv()
        second[1].wait_recv()
        crossing[8].start()
        for n in list(range(2, len(forwards))) + [0]:
            o = (forwards[n][0] - forwards[n][1]) % ZS
            crossing[o].wait_recv()
            converted(o)

        scores = lax.dot_general(base_q[...], lat_k[...], nt, preferred_element_type=F32) * SCALE2
        maxima = jnp.max(scores, axis=1, keepdims=True)
        weights = jnp.exp2(scores - maxima).astype(BF16)
        lat_stats[...] = jnp.broadcast_to(maxima, (64, HD))
        lat_mixed[...] = jnp.dot(weights, lat_v[...], preferred_element_type=F32)

        head = x * ROWS_Y + y

        def to_device(row, g):
            target = (((row * 2 + core) * ZS + z), g)
            return (
                (row == y) & (core == x_hi) & (g == coal),
                remote(
                    results.at[row, pl.ds(g * 96 if isinstance(g, int) else pl.multiple_of(g * 96, 32), 96)], landed.at[head],
                    o_send.at[row * 4 + g], o_recv.at[head], target,
                ),
            )

        def spread(unit):
            text, latent = unit[:8], unit[8:]
            return jnp.concatenate(([text] * 4 + [latent] * 8) * 4, axis=0)

        def one_row(turn):
            row = lax.rem(y + 1 + turn, YS)
            at_row = pl.ds(pl.multiple_of(row * 16, 16), 16)
            asked = base_q[at_row, :].astype(F32)
            left = spread(asked).astype(BF16)
            full = jnp.concatenate([left, bias_rows[...]], axis=1)
            scores = lax.dot_general(full, text_k[...], nt, preferred_element_type=F32)
            shared = spread(lat_stats[at_row, :])[:, :1]
            maxima = jnp.maximum(jnp.max(scores, axis=1, keepdims=True) * SCALE2, shared)
            weights = jnp.exp2(scores * SCALE2 - maxima).astype(BF16)
            total = jnp.dot(weights, text_v[...], preferred_element_type=F32)
            total = total + jnp.exp2(shared - maxima) * spread(lat_mixed[at_row, :])
            results[row] = (total[:, :HD] / total[:, HD:]).astype(BF16)
            for g in range(4):
                to_self, copy = to_device(row, g)
                if turn < YS - 1:
                    copy.start()
                    continue

                @pl.when(to_self)
                def _():
                    part = results.at[row, pl.ds(g * 96, 96)]
                    pltpu.make_async_copy(part, landed.at[head], o_recv.at[head]).start()

                @pl.when(jnp.logical_not(to_self))
                def _():
                    copy.start()

        for turn in range(YS):
            one_row(turn)

        for copy in second:
            copy.wait_send()
        for copy in crossing:
            copy.wait_send()
        for copy in bias_copies():
            copy.wait_send()

        def drained(step, _):
            to_self, copy = to_device(lax.div(step, 4), lax.rem(step, 4))

            @pl.when(jnp.logical_not(to_self))
            def _():
                copy.wait_send()

            return 0

        lax.fori_loop(0, 16, drained, 0)

    for n in range(len(SHIFTS)):
        for y_to in range(ROWS_Y):
            if SHIFTS[n]:
                remote(*rows_to(n, y_to)).wait_send()
            else:

                @pl.when(jnp.logical_not(in_own & (y == y_to)))
                def _():
                    remote(*rows_to(n, y_to)).wait_send()
                    remote(*queries_to(y_to)).wait_send()

    for head in range(ROWS_Y * XS):
        pltpu.make_async_copy(landed.at[head], landed.at[head], o_recv.at[head]).wait()


def laid_out(landed, out_t, out_l):
    for head in range(ROWS_Y * XS):
        cols = pl.ds(head * HD, HD)
        for pair in range(4):
            unit = widened(landed[head, pair * 8 : pair * 8 + 8, :])
            out_t[2 * pair, :, cols] = unit[:4].astype(BF16)
            out_t[2 * pair + 1, :, cols] = unit[4:].astype(BF16)
        for c in range(8):
            out_l[c, :, cols] = landed[head, 32 + c * 8 : 40 + c * 8, :]


def per_device(lat_q, lat_k, lat_v, txt_q, txt_k, txt_v, span_ids, coal_bits):
    vmem = pl.BlockSpec(memory_space=pltpu.VMEM)
    dma = pltpu.SemaphoreType.DMA
    landed = pl.pallas_call(
        kernel,
        out_shape=pltpu.VMEM((12, 96, HD), BF16),
        in_specs=[pl.BlockSpec(memory_space=pl.ANY)] * 8,
        out_specs=vmem,
        scratch_shapes=[
            pltpu.SMEM((4,), jnp.int32), pltpu.SMEM((8,), jnp.int32),
            pltpu.VMEM((8, 1536), BF16), pltpu.VMEM((8, 1536), BF16), pltpu.VMEM((8, 1536), BF16),
            pltpu.VMEM((4, 1536), BF16), pltpu.VMEM((4, 1536), BF16), pltpu.VMEM((4, 1536), BF16),
            pltpu.VMEM((ROWS_Y, PARTS, 4, HD), BF16),
            pltpu.VMEM((ROWS_Y, 3, 4, HD), BF16),
            pltpu.VMEM((YS, 3, 4, HD), BF16),
            pltpu.VMEM((4, 8, HD), BF16),
            pltpu.VMEM((ZS, 2, YS * PARTS, 4, HD), BF16),
            pltpu.VMEM((512, 2 * HD), BF16),
            pltpu.VMEM((512, 2 * HD), BF16),
            pltpu.VMEM((1024, HD), BF16),
            pltpu.VMEM((1024, 2 * HD), BF16),
            pltpu.VMEM((384, HD), BF16),
            pltpu.VMEM((64, HD), BF16),
            pltpu.VMEM((64, HD), F32),
            pltpu.VMEM((64, 2 * HD), F32),
            pltpu.VMEM((YS, 384, HD), BF16),
            dma((8,)), dma((21,)), dma((28,)), dma((3,)), dma((4,)), dma((3,)), dma((4,)),
            dma((10,)), dma((10,)), dma((16,)), dma((16,)), dma((16,)), dma((12,)),
        ],
        compiler_params=pltpu.CompilerParams(collective_id=0, has_side_effects=True),
        name="coalition_attention",
    )(span_ids, coal_bits, lat_q, lat_k, lat_v, txt_q, txt_k, txt_v)
    return pl.pallas_call(
        laid_out,
        out_shape=(jax.ShapeDtypeStruct((8, 4, 1536), BF16), jax.ShapeDtypeStruct((8, 8, 1536), BF16)),
        in_specs=[vmem],
        out_specs=(vmem, vmem),
        name="laid_out",
    )(landed)


def solution(mesh):
    return jax.shard_map(
        per_device,
        mesh=mesh,
        in_specs=(P("seq", None),) * 6 + (P("seq"), P("coal")),
        out_specs=(P("coal", "seq", None), P("coal", "seq", None)),
        check_vma=False,
    )
```

time: 50.8 us -> 43.8 us (0.86)
  the two profiles are of different devices: /device:TPU:63 before, /device:TPU:1 now
where the time goes in v2:
time: 43.8 us; the launch traced here: 43.5 us
  Pallas kernels  42.2 us (96%)
  local copies, waits for them, and re-layouts  0.7 us (2%)
  between operations  0.65 us (1%)
    pallas_call x1, Pallas kernels, per_device(): pl.pallas_call(kernel, out_shape=pltpu.VMEM((12, 96, HD), BF16), in_specs...  40.5 us
    pallas_call x1, Pallas kernels, per_device(): pl.pallas_call(laid_out, out_shape=(jax.ShapeDtypeStruct((8, 4, 1536), BF...  1.73 us

profile of v2, /device:TPU:1, one launch (start us, length us, event | category | flops | bytes accessed | tf_op | source)
XLA Modules:
  0.0 43.5 jit_solution(17084016782575698001)
XLA Ops:
  0.6 40.5 %coalition_attention.1.landed = bf16[12,96,128]{2,1,0:T(8,128)(2,1)S(1)} custom-call(s32[4]{0:T(128)} %spans_in.1, s32[8]{0:T(128)} %bits_in.1, bf16[8,1536]{1,0:T(8,128)(2,1)} %lq_in.1, bf16[8,1536]{1,0:T(8,128)(2,1)} %lk_in.1, bf16[8,1536]{1,0:T(8,128)(2,1)} %lv_in.1, bf16[4,1536]{1,0:T(4,128)(2,1)} %tq_in.1, bf16[4,1536]{1,0:T(4,128)(2,1)} %tk_in.1, ...), custom_call_target="tpu_custom_call" | custom-call | tf_op jit(solution)/shard_map/coalition_attention/pallas_call | solution.py:353
  41.1 0.0 copy-start
  41.1 0.7 %copy-done = bf16[12,96,128]{2,1,0:T(8,128)(2,1)} copy-done((bf16[12,96,128]{2,1,0:T(8,128)(2,1)}, bf16[12,96,128]{2,1,0:T(8,128)(2,1)S(1)}, u32[]{:S(2)}) %copy-start) | copy-done | bytes 294936
  41.8 1.7 %laid_out.1 = (bf16[8,4,1536]{2,1,0:T(4,128)(2,1)}, bf16[8,8,1536]{2,1,0:T(8,128)(2,1)}) custom-call(bf16[12,96,128]{2,1,0:T(8,128)(2,1)} %copy-done), custom_call_target="tpu_custom_call" | custom-call | tf_op jit(solution)/shard_map/laid_out/pallas_call | solution.py:382
Async XLA Ops:
  41.1 0.7 %copy-start = (bf16[12,96,128]{2,1,0:T(8,128)(2,1)}, bf16[12,96,128]{2,1,0:T(8,128)(2,1)S(1)}, u32[]{:S(2)}) copy-start(bf16[12,96,128]{2,1,0:T(8,128)(2,1)S(1)} %coalition_attention.1.landed) | copy-start | bytes 884740

commit v3 on v2

--- a/solution.py
+++ b/solution.py
@@ -24,10 +24,6 @@
 def place():
     seq, coal = lax.axis_index("seq"), lax.axis_index("coal")
     return lax.div(seq, 32), lax.rem(lax.div(seq, 16), 2), lax.rem(seq, 16), lax.div(coal, 2), lax.rem(coal, 2)
-
-
-def device(y, x, z, core):
-    return ((y * 2 + lax.div(x, 2)) * ZS + z, lax.rem(x, 2) * 2 + core)
 
 
 def widened(unit):
@@ -45,8 +41,39 @@
     coal = x_lo * 2 + core
     active = y < ROWS_Y
 
+    z_at = {shift: lax.rem(z + shift + ZS, ZS) for shift in (0, 1, 2, 3, FAR, -1, -2, -3, -FAR)}
+    column = y * 32 + x_hi * 16
+
     def at_z(shift):
-        return device(y, x, lax.rem(z + shift + ZS, ZS), core)
+        return (column + z_at[shift], coal)
+
+    barrier = pltpu.get_barrier_semaphore()
+
+    def greet(partner):
+        pl.semaphore_signal(barrier, inc=1, device_id=partner, device_id_type=MESH)
+
+    in_pair = core == x_hi
+    step_x = jnp.where(x_lo == 0, XS - 1, 1)
+    x_from = jnp.where(in_pair, x, lax.rem(x + step_x, XS))
+    coal_from = lax.rem(x_from, 2) * 2 + jnp.where(in_pair, 0, 1)
+    pair_from = lax.div(x_from, 2) * 16
+    this = column + z
+    others = ((this, x_lo * 2 + 1 - core), (this, (1 - x_lo) * 2 + core), (this, (1 - x_lo) * 2 + 1 - core))
+
+    @pl.when(active)
+    def _():
+        for shift in SHIFTS:
+            for y_from in range(YS):
+                greet((pair_from + z_at[-shift] + y_from * 32, coal_from))
+        for shift in (1, 2, 3):
+            greet(at_z(shift))
+            greet(at_z(-shift))
+        for other in others:
+            greet(other)
+
+    for y_from in range(ROWS_Y):
+        for x_of in range(XS):
+            greet((z + (y_from * 32 + x_of // 2 * 16), x_hi + x_of % 2 * 2))
 
     loads = [
         pltpu.make_async_copy(src, dst, in_sem.at[n])
@@ -57,49 +84,15 @@
     for load in loads:
         load.start()
 
-    barrier = pltpu.get_barrier_semaphore()
-
-    def greet(partner):
-        pl.semaphore_signal(barrier, inc=1, device_id=partner, device_id_type=MESH)
-
-    x_from = jnp.where(core == x_hi, x, jnp.where(x_lo == 0, lax.rem(x + 3, XS), lax.rem(x + 1, XS)))
-    core_from = jnp.where(core == x_hi, 0, 1)
-    other_chip = x_hi * 2 + 1 - x_lo
-    others = (device(y, x, z, 1 - core), device(y, other_chip, z, core), device(y, other_chip, z, 1 - core))
-
-    @pl.when(active)
-    def _():
-        for shift in SHIFTS:
-            for y_from in range(YS):
-                source = device(jnp.int32(y_from), x_from, lax.rem(z - shift + ZS, ZS), core_from)
-                if shift:
-                    greet(source)
-                else:
-
-                    @pl.when(jnp.logical_not((y == y_from) & (core == x_hi) & (core == 0)))
-                    def _():
-                        greet(source)
-
-        for shift in (1, 2, 3):
-            greet(at_z(shift))
-            greet(at_z(-shift))
-        for other in others:
-            greet(other)
-
-    for y_from in range(ROWS_Y):
-        for x_of in range(XS):
-
-            @pl.when(jnp.logical_not((y == y_from) & (x == x_of) & (core == x_hi)))
-            def _():
-                greet(device(jnp.int32(y_from), jnp.int32(x_of), z, x_hi))
-
     for load in loads:
         load.wait()
 
     sub = lax.broadcasted_iota(jnp.int32, (8, HD), 0)
     lane = lax.broadcasted_iota(jnp.int32, (8, HD), 1)
     upper = sub < 4
-    x_to = jnp.where(core == 0, x, jnp.where(x_lo == 0, lax.rem(x + 3, XS), lax.rem(x + 1, XS)))
+    x_to = jnp.where(core == 0, x, lax.rem(x + step_x, XS))
+    pair_to = lax.div(x_to, 2) * 16
+    coal_to = lax.rem(x_to, 2) * 2 + x_hi
     span = jnp.zeros((8, HD), jnp.int32)
     for row in range(4):
         span = jnp.where(sub == row, spans[row], span)
@@ -124,9 +117,7 @@
     lat_v[:, HD:] = jnp.ones((1024, HD), BF16)
 
     in_own = (core == 0) & (x_hi == 0) & active
-    awaited = len(SHIFTS) * ROWS_Y - in_own.astype(jnp.int32)
-    mine = 6 + 3 + 16 - (core == x_hi).astype(jnp.int32)
-    pl.semaphore_wait(barrier, awaited + jnp.where(active, mine, 0))
+    pl.semaphore_wait(barrier, len(SHIFTS) * ROWS_Y + jnp.where(active, 6 + 3 + 16, 0))
 
     def remote(src, dst, send, recv, target):
         return pltpu.make_async_remote_copy(
@@ -134,12 +125,12 @@
         )
 
     def rows_to(n, y_to):
-        target = device(jnp.int32(y_to), x_to, lax.rem(z + SHIFTS[n] + ZS, ZS), x_hi)
+        target = (pair_to + z_at[SHIFTS[n]] + y_to * 32, coal_to)
         there = gathered.at[-SHIFTS[n] % ZS, x_hi, pl.ds(y * PARTS, PARTS)]
         return (own.at[y_to], there, s_send.at[n * ROWS_Y + y_to], s_recv.at[n * YS + y], target)
 
     def queries_to(y_to):
-        target = device(jnp.int32(y_to), x_to, z, x_hi)
+        target = (pair_to + z + y_to * 32, coal_to)
         return (own_q.at[y_to], queries.at[y], q_send.at[y_to], q_recv.at[y], target)
 
     def maybe_own(y_to, copy):
@@ -257,13 +248,14 @@
         lat_mixed[...] = jnp.dot(weights, lat_v[...], preferred_element_type=F32)
 
         head = x * ROWS_Y + y
+        near_last = jnp.where(in_pair, x_lo, jnp.where(x_lo == 0, 1, 0))
 
         def to_device(row, g):
             target = (((row * 2 + core) * ZS + z), g)
             return (
                 (row == y) & (core == x_hi) & (g == coal),
                 remote(
-                    results.at[row, pl.ds(g * 96 if isinstance(g, int) else pl.multiple_of(g * 96, 32), 96)], landed.at[head],
+                    results.at[row, pl.ds(g * 12, 12)], landed.at[head],
                     o_send.at[row * 4 + g], o_recv.at[head], target,
                 ),
             )
@@ -273,7 +265,7 @@
             return jnp.concatenate(([text] * 4 + [latent] * 8) * 4, axis=0)
 
         def one_row(turn):
-            row = lax.rem(y + 1 + turn, YS)
+            row = lax.rem(y + (2, 1, 3, 0)[turn], YS)
             at_row = pl.ds(pl.multiple_of(row * 16, 16), 16)
             asked = base_q[at_row, :].astype(F32)
             left = spread(asked).astype(BF16)
@@ -284,8 +276,9 @@
             weights = jnp.exp2(scores * SCALE2 - maxima).astype(BF16)
             total = jnp.dot(weights, text_v[...], preferred_element_type=F32)
             total = total + jnp.exp2(shared - maxima) * spread(lat_mixed[at_row, :])
-            results[row] = (total[:, :HD] / total[:, HD:]).astype(BF16)
-            for g in range(4):
+            results[row] = (total[:, :HD] / total[:, HD:]).reshape(48, 8, HD).astype(BF16)
+            for near in range(4):
+                g = lax.rem(2 * near_last + near + 2, 4)
                 to_self, copy = to_device(row, g)
                 if turn < YS - 1:
                     copy.start()
@@ -293,7 +286,7 @@
 
                 @pl.when(to_self)
                 def _():
-                    part = results.at[row, pl.ds(g * 96, 96)]
+                    part = results.at[row, pl.ds(g * 12, 12)]
                     pltpu.make_async_copy(part, landed.at[head], o_recv.at[head]).start()
 
                 @pl.when(jnp.logical_not(to_self))
@@ -336,15 +329,21 @@
         pltpu.make_async_copy(landed.at[head], landed.at[head], o_recv.at[head]).wait()
 
 
-def laid_out(landed, out_t, out_l):
+def laid_out(landed, out_t, out_l, text, sems):
+    copies = []
     for head in range(ROWS_Y * XS):
         cols = pl.ds(head * HD, HD)
+        copies.append(pltpu.make_async_copy(landed.at[head, pl.ds(4, 8)], out_l.at[:, :, cols], sems.at[head]))
+        copies[-1].start()
+    for head in range(ROWS_Y * XS):
         for pair in range(4):
-            unit = widened(landed[head, pair * 8 : pair * 8 + 8, :])
-            out_t[2 * pair, :, cols] = unit[:4].astype(BF16)
-            out_t[2 * pair + 1, :, cols] = unit[4:].astype(BF16)
-        for c in range(8):
-            out_l[c, :, cols] = landed[head, 32 + c * 8 : 40 + c * 8, :]
+            unit = widened(landed[head, pair])
+            text[2 * pair, :, head * HD : (head + 1) * HD] = unit[:4].astype(BF16)
+            text[2 * pair + 1, :, head * HD : (head + 1) * HD] = unit[4:].astype(BF16)
+    copies.append(pltpu.make_async_copy(text, out_t, sems.at[12]))
+    copies[-1].start()
+    for copy in copies:
+        copy.wait()
 
 
 def per_device(lat_q, lat_k, lat_v, txt_q, txt_k, txt_v, span_ids, coal_bits):
@@ -352,7 +351,7 @@
     dma = pltpu.SemaphoreType.DMA
     landed = pl.pallas_call(
         kernel,
-        out_shape=pltpu.VMEM((12, 96, HD), BF16),
+        out_shape=pltpu.VMEM((12, 12, 8, HD), BF16),
         in_specs=[pl.BlockSpec(memory_space=pl.ANY)] * 8,
         out_specs=vmem,
         scratch_shapes=[
@@ -372,7 +371,7 @@
             pltpu.VMEM((64, HD), BF16),
             pltpu.VMEM((64, HD), F32),
             pltpu.VMEM((64, 2 * HD), F32),
-            pltpu.VMEM((YS, 384, HD), BF16),
+            pltpu.VMEM((YS, 48, 8, HD), BF16),
             dma((8,)), dma((21,)), dma((28,)), dma((3,)), dma((4,)), dma((3,)), dma((4,)),
             dma((10,)), dma((10,)), dma((16,)), dma((16,)), dma((16,)), dma((12,)),
         ],
@@ -383,9 +382,10 @@
         laid_out,
         out_shape=(jax.ShapeDtypeStruct((8, 4, 1536), BF16), jax.ShapeDtypeStruct((8, 8, 1536), BF16)),
         in_specs=[vmem],
-        out_specs=(vmem, vmem),
+        out_specs=(pl.BlockSpec(memory_space=pl.ANY),) * 2,
+        scratch_shapes=[pltpu.VMEM((8, 4, 1536), BF16), dma((13,))],
         name="laid_out",
-    )(landed)
+    )(pltpu.with_memory_space_constraint(landed, pltpu.VMEM))
 
 
 def solution(mesh):

time: 43.8 us -> 41.4 us (0.945)
  Pallas kernels: 42.2 us -> 40.6 us
  local copies, waits for them, and re-layouts: 0.7 us -> 0 us
    pallas_call x1, Pallas kernels: 1.73 us -> 0.82 us  [per_device(): pl.pallas_call(laid_out, out_shape=(jax.ShapeDtypeStruct((8, 4, 1536), BF...]
    pallas_call x1, Pallas kernels: 40.5 us -> 39.7 us  [per_device(): pl.pallas_call(kernel, out_shape=pltpu.VMEM((12, 12, 8, HD), BF16), in_sp...]
    unnamed x2 -> x0, local copies, waits for them, and re-layouts: 0.7 us -> none
where the time goes in v3:
time: 41.4 us; the launch traced here: 41.2 us
  Pallas kernels  40.6 us (98%)
  between operations  0.64 us (2%)
    pallas_call x1, Pallas kernels, per_device(): pl.pallas_call(kernel, out_shape=pltpu.VMEM((12, 12, 8, HD), BF16), in_sp...  39.7 us

profile of v3, /device:TPU:1, one launch (start us, length us, event | category | flops | bytes accessed | tf_op | source)
XLA Modules:
  0.0 41.2 jit_solution(16770652816889955515)
XLA Ops:
  0.6 39.7 %coalition_attention.1.landed = bf16[12,12,8,128]{3,2,1,0:T(8,128)(2,1)S(1)} custom-call(s32[4]{0:T(128)} %spans_in.1, s32[8]{0:T(128)} %bits_in.1, bf16[8,1536]{1,0:T(8,128)(2,1)} %lq_in.1, bf16[8,1536]{1,0:T(8,128)(2,1)} %lk_in.1, bf16[8,1536]{1,0:T(8,128)(2,1)} %lv_in.1, bf16[4,1536]{1,0:T(4,128)(2,1)} %tq_in.1, bf16[4,1536]{1,0:T(4,128)(2,1)} %tk_in.1, ...), custom_call_target="tpu_custom_call" | custom-call | tf_op jit(solution)/shard_map/coalition_attention/pallas_call | solution.py:352
  40.4 0.8 %laid_out.1 = (bf16[8,4,1536]{2,1,0:T(4,128)(2,1)}, bf16[8,8,1536]{2,1,0:T(8,128)(2,1)}) custom-call(bf16[12,12,8,128]{3,2,1,0:T(8,128)(2,1)S(1)} %coalition_attention.1.landed), custom_call_target="tpu_custom_call" | custom-call | tf_op jit(solution)/shard_map/laid_out/pallas_call | solution.py:381

commit v4 on v3

--- a/solution.py
+++ b/solution.py
@@ -18,7 +18,7 @@
 HIDDEN = -1e30
 PARTS = 7
 FAR = 5
-SHIFTS = (FAR, -FAR, 2, -2, 1, -1, 0)
+SHIFTS = (FAR, -FAR, 3, -3, 2, -2, 1, -1, 0)
 
 
 def place():
@@ -171,7 +171,7 @@
     half = whole // 2
     forwards = [
         (FAR, -3, half, whole - half), (-FAR, 3, 0, half),
-        (FAR, 2), (FAR, -2), (FAR, 1), (FAR, -1), (-FAR, 2), (-FAR, -2), (-FAR, 1), (-FAR, -1),
+        (FAR, -2), (-FAR, 2), (FAR, 1), (FAR, -1), (-FAR, 1), (-FAR, -1),
     ]
 
     def direct_in(n):
@@ -372,8 +372,8 @@
             pltpu.VMEM((64, HD), F32),
             pltpu.VMEM((64, 2 * HD), F32),
             pltpu.VMEM((YS, 48, 8, HD), BF16),
-            dma((8,)), dma((21,)), dma((28,)), dma((3,)), dma((4,)), dma((3,)), dma((4,)),
-            dma((10,)), dma((10,)), dma((16,)), dma((16,)), dma((16,)), dma((12,)),
+            dma((8,)), dma((27,)), dma((36,)), dma((3,)), dma((4,)), dma((3,)), dma((4,)),
+            dma((8,)), dma((8,)), dma((16,)), dma((16,)), dma((16,)), dma((12,)),
         ],
         compiler_params=pltpu.CompilerParams(collective_id=0, has_side_effects=True),
         name="coalition_attention",

time: 41.4 us -> 40.9 us (0.988)
  Pallas kernels: 40.6 us -> 40.1 us
    pallas_call x1, Pallas kernels: 39.7 us -> 39.3 us  [per_device(): pl.pallas_call(kernel, out_shape=pltpu.VMEM((12, 12, 8, HD), BF16), in_sp...]
where the time goes in v4:
time: 40.9 us; the launch traced here: 40.7 us
  Pallas kernels  40.1 us (98%)
  between operations  0.64 us (2%)
    pallas_call x1, Pallas kernels, per_device(): pl.pallas_call(kernel, out_shape=pltpu.VMEM((12, 12, 8, HD), BF16), in_sp...  39.3 us
    pallas_call x1, Pallas kernels, per_device(): pl.pallas_call(laid_out, out_shape=(jax.ShapeDtypeStruct((8, 4, 1536), BF...  0.82 us

profile of v4, /device:TPU:1, one launch (start us, length us, event | category | flops | bytes accessed | tf_op | source)
XLA Modules:
  0.0 40.7 jit_solution(5099254624881875025)
XLA Ops:
  0.6 39.3 %coalition_attention.1.landed = bf16[12,12,8,128]{3,2,1,0:T(8,128)(2,1)S(1)} custom-call(s32[4]{0:T(128)} %spans_in.1, s32[8]{0:T(128)} %bits_in.1, bf16[8,1536]{1,0:T(8,128)(2,1)} %lq_in.1, bf16[8,1536]{1,0:T(8,128)(2,1)} %lk_in.1, bf16[8,1536]{1,0:T(8,128)(2,1)} %lv_in.1, bf16[4,1536]{1,0:T(4,128)(2,1)} %tq_in.1, bf16[4,1536]{1,0:T(4,128)(2,1)} %tk_in.1, ...), custom_call_target="tpu_custom_call" | custom-call | tf_op jit(solution)/shard_map/coalition_attention/pallas_call | solution.py:352
  39.9 0.8 %laid_out.1 = (bf16[8,4,1536]{2,1,0:T(4,128)(2,1)}, bf16[8,8,1536]{2,1,0:T(8,128)(2,1)}) custom-call(bf16[12,12,8,128]{3,2,1,0:T(8,128)(2,1)S(1)} %coalition_attention.1.landed), custom_call_target="tpu_custom_call" | custom-call | tf_op jit(solution)/shard_map/laid_out/pallas_call | solution.py:381

commit v5 on v4

--- a/solution.py
+++ b/solution.py
@@ -18,7 +18,7 @@
 HIDDEN = -1e30
 PARTS = 7
 FAR = 5
-SHIFTS = (FAR, -FAR, 3, -3, 2, -2, 1, -1, 0)
+SHIFTS = (0, FAR, -FAR)
 
 
 def place():
@@ -145,7 +145,7 @@
         def _():
             remote(src, dst, send, recv, target).start()
 
-    for n in range(len(SHIFTS)):
+    for n in (1, 2, 0):
         for y_to in range(ROWS_Y):
             if SHIFTS[n]:
                 remote(*rows_to(n, y_to)).start()
@@ -170,6 +170,7 @@
 
     half = whole // 2
     forwards = [
+        (0, 3), (0, -3), (0, 2), (0, -2), (0, 1), (0, -1),
         (FAR, -3, half, whole - half), (-FAR, 3, 0, half),
         (FAR, -2), (-FAR, 2), (FAR, 1), (FAR, -1), (-FAR, 1), (-FAR, -1),
     ]
@@ -202,15 +203,20 @@
             copy.start()
         second = [ring(n, *f) for n, f in enumerate(forwards)]
         crossing = [across(o) for o in range(ZS)]
-        for n in (0, 1):
+        def arrived(n):
+            second[n].wait_recv()
+            offset = (forwards[n][0] - forwards[n][1]) % ZS
+            if offset != 8:
+                crossing[offset].start()
+            return offset
+
+        for n in range(len(SHIFTS)):
             direct_in(n)
             for f, copy in zip(forwards, second):
                 if f[0] == -SHIFTS[n]:
                     copy.start()
             crossing[-SHIFTS[n] % ZS].start()
-        for n in range(2, len(SHIFTS)):
-            direct_in(n)
-            crossing[-SHIFTS[n] % ZS].start()
+        early = [0, FAR, ZS - FAR] + [arrived(n) for n in (4, 5, 2, 3, 0, 1)]
 
         for n in range(YS):
             pltpu.make_async_copy(queries.at[n], queries.at[n], q_recv.at[n]).wait()
@@ -227,19 +233,16 @@
             parts = [jnp.where(upper, rows[2 * p], rows[2 * p + 1]) for p in range(4)]
             parts += [jnp.broadcast_to(row, (8, HD)) for row in rows]
             bias_rows[pl.ds(g * 96, 96), :] = jnp.concatenate(parts, axis=0).astype(BF16)
-        for shift in SHIFTS:
-            crossing[-shift % ZS].wait_recv()
-            converted(-shift % ZS)
-        for n in range(2, len(forwards)):
-            second[n].wait_recv()
-            crossing[(forwards[n][0] - forwards[n][1]) % ZS].start()
-        second[0].wait_recv()
-        second[1].wait_recv()
+        for offset in early:
+            crossing[offset].wait_recv()
+            converted(offset)
+        late = [arrived(n) for n in range(8, 14)] + [8]
+        second[6].wait_recv()
+        second[7].wait_recv()
         crossing[8].start()
-        for n in list(range(2, len(forwards))) + [0]:
-            o = (forwards[n][0] - forwards[n][1]) % ZS
-            crossing[o].wait_recv()
-            converted(o)
+        for offset in late:
+            crossing[offset].wait_recv()
+            converted(offset)
 
         scores = lax.dot_general(base_q[...], lat_k[...], nt, preferred_element_type=F32) * SCALE2
         maxima = jnp.max(scores, axis=1, keepdims=True)
@@ -372,8 +375,8 @@
             pltpu.VMEM((64, HD), F32),
             pltpu.VMEM((64, 2 * HD), F32),
             pltpu.VMEM((YS, 48, 8, HD), BF16),
-            dma((8,)), dma((27,)), dma((36,)), dma((3,)), dma((4,)), dma((3,)), dma((4,)),
-            dma((8,)), dma((8,)), dma((16,)), dma((16,)), dma((16,)), dma((12,)),
+            dma((8,)), dma((9,)), dma((12,)), dma((3,)), dma((4,)), dma((3,)), dma((4,)),
+            dma((14,)), dma((14,)), dma((16,)), dma((16,)), dma((16,)), dma((12,)),
         ],
         compiler_params=pltpu.CompilerParams(collective_id=0, has_side_effects=True),
         name="coalition_attention",

time: 40.9 us -> 41 us (level)
  no operation moved by 1% of the time
where the time goes in v5:
time: 41 us; the launch traced here: 40.8 us
  Pallas kernels  40.1 us (98%)
  between operations  0.64 us (2%)
    pallas_call x1, Pallas kernels, per_device(): pl.pallas_call(kernel, out_shape=pltpu.VMEM((12, 12, 8, HD), BF16), in_sp...  39.3 us
    pallas_call x1, Pallas kernels, per_device(): pl.pallas_call(laid_out, out_shape=(jax.ShapeDtypeStruct((8, 4, 1536), BF...  0.82 us

profile of v5, /device:TPU:1, one launch (start us, length us, event | category | flops | bytes accessed | tf_op | source)
XLA Modules:
  0.0 40.8 jit_solution(15582719604829219392)
XLA Ops:
  0.6 39.3 %coalition_attention.1.landed = bf16[12,12,8,128]{3,2,1,0:T(8,128)(2,1)S(1)} custom-call(s32[4]{0:T(128)} %spans_in.1, s32[8]{0:T(128)} %bits_in.1, bf16[8,1536]{1,0:T(8,128)(2,1)} %lq_in.1, bf16[8,1536]{1,0:T(8,128)(2,1)} %lk_in.1, bf16[8,1536]{1,0:T(8,128)(2,1)} %lv_in.1, bf16[4,1536]{1,0:T(4,128)(2,1)} %tq_in.1, bf16[4,1536]{1,0:T(4,128)(2,1)} %tk_in.1, ...), custom_call_target="tpu_custom_call" | custom-call | tf_op jit(solution)/shard_map/coalition_attention/pallas_call | solution.py:355
  40.0 0.8 %laid_out.1 = (bf16[8,4,1536]{2,1,0:T(4,128)(2,1)}, bf16[8,8,1536]{2,1,0:T(8,128)(2,1)}) custom-call(bf16[12,12,8,128]{3,2,1,0:T(8,128)(2,1)S(1)} %coalition_attention.1.landed), custom_call_target="tpu_custom_call" | custom-call | tf_op jit(solution)/shard_map/laid_out/pallas_call | solution.py:384

commit v6 on v4

--- a/solution.py
+++ b/solution.py
@@ -202,6 +202,21 @@
             copy.start()
         second = [ring(n, *f) for n, f in enumerate(forwards)]
         crossing = [across(o) for o in range(ZS)]
+        for n in range(YS):
+            pltpu.make_async_copy(queries.at[n], queries.at[n], q_recv.at[n]).wait()
+            asked = [widened(queries[n, m]) for m in (0, 0, 1, 2)]
+            base_q[pl.ds(n * 16, 16), :] = jnp.concatenate(asked, axis=0).astype(BF16)
+        for g in range(4):
+
+            @pl.when(coal != g)
+            def _():
+                pltpu.make_async_copy(biases.at[g], biases.at[g], b_recv.at[g]).wait()
+
+            unit = widened(biases[g])
+            rows = [unit[c : c + 1, :] for c in range(8)]
+            parts = [jnp.where(upper, rows[2 * p], rows[2 * p + 1]) for p in range(4)]
+            parts += [jnp.broadcast_to(row, (8, HD)) for row in rows]
+            bias_rows[pl.ds(g * 96, 96), :] = jnp.concatenate(parts, axis=0).astype(BF16)
         for n in (0, 1):
             direct_in(n)
             for f, copy in zip(forwards, second):
@@ -212,31 +227,16 @@
             direct_in(n)
             crossing[-SHIFTS[n] % ZS].start()
 
-        for n in range(YS):
-            pltpu.make_async_copy(queries.at[n], queries.at[n], q_recv.at[n]).wait()
-            asked = [widened(queries[n, m]) for m in (0, 0, 1, 2)]
-            base_q[pl.ds(n * 16, 16), :] = jnp.concatenate(asked, axis=0).astype(BF16)
-        for g in range(4):
-
-            @pl.when(coal != g)
-            def _():
-                pltpu.make_async_copy(biases.at[g], biases.at[g], b_recv.at[g]).wait()
-
-            unit = widened(biases[g])
-            rows = [unit[c : c + 1, :] for c in range(8)]
-            parts = [jnp.where(upper, rows[2 * p], rows[2 * p + 1]) for p in range(4)]
-            parts += [jnp.broadcast_to(row, (8, HD)) for row in rows]
-            bias_rows[pl.ds(g * 96, 96), :] = jnp.concatenate(parts, axis=0).astype(BF16)
         for shift in SHIFTS:
             crossing[-shift % ZS].wait_recv()
             converted(-shift % ZS)
-        for n in range(2, len(forwards)):
+        for n in (4, 5, 6, 7, 2, 3):
             second[n].wait_recv()
             crossing[(forwards[n][0] - forwards[n][1]) % ZS].start()
         second[0].wait_recv()
         second[1].wait_recv()
         crossing[8].start()
-        for n in list(range(2, len(forwards))) + [0]:
+        for n in (4, 5, 6, 7, 2, 3, 0):
             o = (forwards[n][0] - forwards[n][1]) % ZS
             crossing[o].wait_recv()
             converted(o)

time: 40.9 us -> 40.9 us (level)
  no operation moved by 1% of the time
where the time goes in v6:
time: 40.9 us; the launch traced here: 40.7 us
  Pallas kernels  40.1 us (98%)
  between operations  0.64 us (2%)
    pallas_call x1, Pallas kernels, per_device(): pl.pallas_call(kernel, out_shape=pltpu.VMEM((12, 12, 8, HD), BF16), in_sp...  39.3 us
    pallas_call x1, Pallas kernels, per_device(): pl.pallas_call(laid_out, out_shape=(jax.ShapeDtypeStruct((8, 4, 1536), BF...  0.82 us

profile of v6, /device:TPU:1, one launch (start us, length us, event | category | flops | bytes accessed | tf_op | source)
XLA Modules:
  0.0 40.7 jit_solution(8211337268668196370)
XLA Ops:
  0.6 39.3 %coalition_attention.1.landed = bf16[12,12,8,128]{3,2,1,0:T(8,128)(2,1)S(1)} custom-call(s32[4]{0:T(128)} %spans_in.1, s32[8]{0:T(128)} %bits_in.1, bf16[8,1536]{1,0:T(8,128)(2,1)} %lq_in.1, bf16[8,1536]{1,0:T(8,128)(2,1)} %lk_in.1, bf16[8,1536]{1,0:T(8,128)(2,1)} %lv_in.1, bf16[4,1536]{1,0:T(4,128)(2,1)} %tq_in.1, bf16[4,1536]{1,0:T(4,128)(2,1)} %tk_in.1, ...), custom_call_target="tpu_custom_call" | custom-call | tf_op jit(solution)/shard_map/coalition_attention/pallas_call | solution.py:352
  39.9 0.8 %laid_out.1 = (bf16[8,4,1536]{2,1,0:T(4,128)(2,1)}, bf16[8,8,1536]{2,1,0:T(8,128)(2,1)}) custom-call(bf16[12,12,8,128]{3,2,1,0:T(8,128)(2,1)S(1)} %coalition_attention.1.landed), custom_call_target="tpu_custom_call" | custom-call | tf_op jit(solution)/shard_map/laid_out/pallas_call | solution.py:381
